TPU v7x, 256 devices: a whole 4x4x8 slice. The times are simulated.
256 devices in a mesh: kv: 4 (over y), blk: 64 (over z, x, core).
Axes of the slice: x: 4, y: 4, z: 8, core: 2. Of those that a mesh axis runs over, the one named last changes fastest.
Arguments:
- queries: bfloat16 [64, 2560], P('blk', 'kv'), may hold values from -104 to 104
- kv_pool: bfloat16 [8192, 2, 64, 512], P('blk', None, None, 'kv'), may hold values from -4 to 4
- block_table: int32 [64, 256], replicated, may hold values from -1 to 8191, as said below
- lengths: int32 [64], replicated, may hold values from 2 to 16384, as said below
- residual: bfloat16 [64, 2560], P('blk', 'kv'), may hold values from -6 to 6
- out_weight: bfloat16 [2560, 2560], P('kv'), may hold values from -0.125 to 0.125
- norm_gain: bfloat16 [2560], replicated, may hold values from 0.5 to 1.5
- qkv_weight: bfloat16 [2560, 3584], P(None, 'kv'), may hold values from -0.125 to 0.125
Outputs:
- stream_out: bfloat16 [64, 2560], P('blk', 'kv')
- next_qkv: bfloat16 [64, 3584], P('blk', 'kv')
Inputs may be any that keep to these rules, and one draw needn't show every extreme that they name: `block_table`: row r names ceil(lengths[r] / 64) pool blocks, then -1; different rows and slots name different blocks. `lengths`: some request has exactly 16384 tokens.
All inputs are finite; a program needn't handle non-finite values.
Results may differ from a plain program's by a relative error of at most 0.0065.
Values may be sent and summed in bfloat16 or wider, within the bound.
A program may use at most 64 MiB of HBM per device.

v0:
```python
import jax
import jax.numpy as jnp
from jax import lax
from jax.sharding import PartitionSpec as P

HEAD = 128


def joined(part, axis, combine):
    gathered = jax.tree.map(lambda a: lax.all_gather(a, axis), part)

    def take(source):
        return jax.tree.map(lambda a: lax.dynamic_index_in_dim(a, source, 0, False), gathered)

    return lax.fori_loop(
        1, lax.axis_size(axis), lambda source, state: combine(state, take(source)), take(0)
    )


def combine_parts(first, second):
    top_a, total_a, out_a = first
    top_b, total_b, out_b = second
    top = jnp.maximum(top_a, top_b)
    scale_a = jnp.exp(top_a - top)
    scale_b = jnp.exp(top_b - top)
    total = scale_a * total_a + scale_b * total_b
    shape = out_a.shape
    group = top.shape[-1]
    out = (
        out_a.reshape(shape[:-1] + (group, -1)) * scale_a[..., None]
        + out_b.reshape(shape[:-1] + (group, -1)) * scale_b[..., None]
    )
    return (top, total, out.reshape(shape))


def per_device(queries, kv_pool, block_table, lengths, residual, out_weight, norm_gain, qkv_weight):
    every_query = lax.all_gather(queries, "blk", axis=0, tiled=True)
    num_req = every_query.shape[0]
    num_blocks = kv_pool.shape[0]
    block = kv_pool.shape[2]
    group = every_query.shape[1] // HEAD
    max_blocks = block_table.shape[1]
    first_block = lax.axis_index("blk") * num_blocks
    local = block_table - first_block
    inside = (local >= 0) & (local < num_blocks)
    target = jnp.where(inside, local, num_blocks).reshape(-1)
    req_ids = jnp.broadcast_to(
        jnp.arange(num_req, dtype=jnp.int32)[:, None], (num_req, max_blocks)
    ).reshape(-1)
    slot_ids = jnp.broadcast_to(
        jnp.arange(max_blocks, dtype=jnp.int32)[None, :], (num_req, max_blocks)
    ).reshape(-1)
    owner = jnp.full((num_blocks,), -1, jnp.int32).at[target].set(req_ids, mode="drop")
    slot = jnp.zeros((num_blocks,), jnp.int32).at[target].set(slot_ids, mode="drop")
    used = owner >= 0
    safe_owner = jnp.maximum(owner, 0)
    block_query = every_query[safe_owner].reshape(num_blocks, group, HEAD)
    keys = kv_pool[:, 0]
    values = kv_pool[:, 1]
    score = jnp.einsum(
        "btd,bgd->btg", keys, block_query, preferred_element_type=jnp.float32
    ) * HEAD ** (-0.5)
    limit = lengths[safe_owner] - slot * block
    valid = (jnp.arange(block)[None, :] < limit[:, None]) & used[:, None]
    score = jnp.where(valid[..., None], score, jnp.float32(-1e30))
    block_max = jnp.max(score, axis=1)
    expo = jnp.exp(score - block_max[:, None, :]) * valid[..., None].astype(jnp.float32)
    block_sum = jnp.sum(expo, axis=1)
    block_out = jnp.einsum(
        "btg,btd->bgd", expo.astype(jnp.bfloat16), values, preferred_element_type=jnp.float32
    )
    onehot = jnp.arange(num_req, dtype=jnp.int32)[:, None] == owner[None, :]
    local_top = jnp.max(jnp.where(onehot[:, :, None], block_max[None], jnp.float32(-1e30)), axis=1)
    weight = jnp.exp(block_max - local_top[safe_owner]) * used[:, None].astype(jnp.float32)
    onehot_float = onehot.astype(jnp.float32)
    local_total = jnp.dot(onehot_float, weight * block_sum, precision=lax.Precision.HIGHEST)
    scaled_out = (weight[..., None] * block_out).reshape(num_blocks, group * HEAD)
    local_out = jnp.dot(onehot_float, scaled_out, precision=lax.Precision.HIGHEST)
    num_dev = lax.axis_size("blk")
    req_dev = num_req // num_dev
    top, total, summed = joined((local_top, local_total, local_out), "blk", combine_parts)
    start = lax.axis_index("blk") * req_dev
    total = lax.dynamic_slice_in_dim(total, start, req_dev, 0)
    summed = lax.dynamic_slice_in_dim(summed, start, req_dev, 0)
    attn = (
        (summed.reshape(req_dev, group, HEAD) / total[..., None])
        .reshape(req_dev, group * HEAD)
        .astype(jnp.bfloat16)
    )
    partial_proj = jnp.dot(attn, out_weight, preferred_element_type=jnp.float32)
    columns = residual.shape[1]
    kv_index = lax.axis_index("kv")
    width = partial_proj.shape[1]
    gain = norm_gain.astype(jnp.float32)
    own_proj = lax.psum_scatter(partial_proj, "kv", scatter_dimension=1, tiled=True)
    hidden = residual.astype(jnp.float32) + own_proj
    squares = lax.psum(jnp.sum(hidden * hidden, axis=1), "kv")
    inverse = lax.rsqrt(squares / width + 1e-05)
    own_gain = lax.dynamic_slice_in_dim(gain, kv_index * columns, columns, 0)
    normed_part = (hidden * inverse[:, None] * own_gain[None, :]).astype(jnp.bfloat16)
    normed = lax.all_gather(normed_part, "kv", axis=1, tiled=True)
    stream_out = hidden.astype(jnp.bfloat16)
    next_qkv = jnp.dot(normed, qkv_weight, preferred_element_type=jnp.float32).astype(jnp.bfloat16)
    return (stream_out, next_qkv)


def solution(mesh):
    placed = (
        P("blk", "kv"),
        P("blk", None, None, "kv"),
        P(),
        P(),
        P("blk", "kv"),
        P("kv", None),
        P(),
        P(None, "kv"),
    )
    return jax.shard_map(
        per_device,
        mesh=mesh,
        in_specs=placed,
        out_specs=(P("blk", "kv"), P("blk", "kv")),
        check_vma=False,
    )
```

profile of v0, /device:TPU:2, one launch (start us, length us, event | category | flops | bytes accessed | tf_op | source)
XLA Modules:
  0.0 574.7 jit_solution(2944230899125286297)
XLA Ops:
  9.1 60.5 %scatter_custom_fusion = s32[128]{0:T(128)S(1)} fusion(s32[16384]{0:T(1024)S(1)} %bitcast.116, s32[16384]{0:T(1024)} %bitcast.119, s32[]{:T(128)} %constant.78.clone.1), kind=kCustom, calls=%fused_computation.67 | custom fusion | bytes 1024 | tf_op jit(solution)/shard_map/scatter | solution.py:53
  70.3 46.6 %all-gather.3 = bf16[64,1,640]{2,1,0:T(2,128)(2,1)S(1)} all-gather(bf16[1,1,640]{2,1,0:T(2,128)(2,1)} %bitcast.121), channel_id=1, replica_groups=mesh['kv'=4,'blk'=64] {'blk'}, dimensions={0}, use_global_device_ids=true | all-gather | bytes 83200 | tf_op jit(solution)/shard_map/all_gather | solution.py:37
  117.0 1.6 gather_fusion
  118.5 1.5 gather_fusion.1
  122.0 60.5 %scatter_custom_fusion.1 = s32[128]{0:T(128)S(1)} fusion(s32[16384]{0:T(1024)S(1)} %bitcast.117, s32[16384]{0:T(1024)} %bitcast.118, s32[]{:T(128)} %constant.77.clone.1), kind=kCustom, calls=%fused_computation.64 | custom fusion | bytes 1024 | tf_op jit(solution)/shard_map/scatter | solution.py:54
  182.7 3.7 fusion.43
  188.9 3.3 fusion.18
  192.2 1.9 copy.49
  194.1 2.0 fusion.28
  196.2 1.4 fusion.22
  197.8 41.9 %all-gather.5 = f32[64,64,5]{1,2,0:T(8,128)S(1)} all-gather(f32[1,64,5]{1,2,0:T(8,128)S(1)} %convolution_bitcast_fusion.1), channel_id=3, replica_groups=mesh['kv'=4,'blk'=64] {'blk'}, dimensions={0}, use_global_device_ids=true | all-gather | bytes 83200 | tf_op jit(solution)/shard_map/all_gather | solution.py:10
  240.5 43.2 %all-gather.4 = f32[64,64,5]{1,2,0:T(8,128)S(1)} all-gather(f32[1,64,5]{1,2,0:T(8,128)S(1)} %bitcast.120), channel_id=2, replica_groups=mesh['kv'=4,'blk'=64] {'blk'}, dimensions={0}, use_global_device_ids=true | all-gather | bytes 83200 | tf_op jit(solution)/shard_map/all_gather | solution.py:10
  286.0 226.0 %while.19 = (s32[]{:T(128)}, f32[64,5]{1,0:T(8,128)}, f32[64,5]{1,0:T(8,128)S(1)}, f32[64,640]{1,0:T(8,128)S(1)}, f32[64,64,5]{1,2,0:T(8,128)}, /*index=5*/f32[6...) while((s32[]{:T(128)}, f32[64,5]{1,0:T(8,128)}, f32[64,5]{1,0:T(8,128)S(1)}, ...), condition=%wide.region_6.7_spmd, body=%wide.region_5.6_spmd.sunk | while | flops 124805 | bytes 1170071 | solution.py:15
  286.9 1.4 fusion.50
  290.5 1.4 fusion.50
  294.1 1.4 fusion.50
  297.6 1.4 fusion.50
  301.2 1.4 fusion.50
  304.8 1.4 fusion.50
  308.4 1.4 fusion.50
  312.0 1.4 fusion.50
  315.6 1.4 fusion.50
  319.1 1.4 fusion.50
  322.7 1.4 fusion.50
  326.3 1.4 fusion.50
  329.9 1.4 fusion.50
  333.5 1.4 fusion.50
  337.1 1.4 fusion.50
  340.7 1.4 fusion.50
  344.3 1.4 fusion.50
  347.9 1.4 fusion.50
  351.5 1.4 fusion.50
  355.1 1.4 fusion.50
  358.7 1.4 fusion.50
  362.3 1.4 fusion.50
  365.9 1.4 fusion.50
  369.5 1.4 fusion.50
  373.1 1.4 fusion.50
  391.0 1.4 fusion.50
  408.9 1.4 fusion.50
  412.5 1.4 fusion.50
  416.1 1.4 fusion.50
  419.6 1.4 fusion.50
  423.2 1.4 fusion.50
  437.6 1.4 fusion.50
  441.2 1.4 fusion.50
  444.8 1.4 fusion.50
  448.4 1.4 fusion.50
  455.5 1.4 fusion.50
  462.7 1.4 fusion.50
  466.3 1.4 fusion.50
  469.9 1.4 fusion.50
  473.5 1.4 fusion.50
  477.1 1.4 fusion.50
  480.7 1.4 fusion.50
  487.9 1.4 fusion.50
  491.4 1.4 fusion.50
  498.6 1.4 fusion.50
  505.8 1.4 fusion.50
  512.1 2.4 convolution_bitcast_fusion
  515.3 24.8 %reduce-scatter.4.cloned.1.call-done = f32[640,1]{1,0:T(8,128)} async-done(((f32[2560,1]{1,0:T(8,128)}), f32[640,1]{1,0:T(8,128)}) %reduce-scatter.4.cloned.1.call-update) | async-done | bytes 2576
  541.8 9.4 %psum.7 = f32[1]{0:T(128)} all-reduce(f32[1]{0:T(128)} %bitcast.16), channel_id=1, replica_groups=mesh['kv'=4,'blk'=64] {'kv'}, use_global_device_ids=true, to_apply=%region_9.10 | all-reduce | flops 1 | bytes 8 | tf_op jit(solution)/shard_map/psum | solution.py:97
  552.5 11.8 %all_gather.31 = bf16[1,2560]{1,0:T(2,128)(2,1)S(1)} all-gather(bf16[1,640]{1,0:T(2,128)(2,1)S(1)} %get-tuple-element.236), channel_id=1, replica_groups=mesh['kv'=4,'blk'=64] {'kv'}, dimensions={1}, use_global_device_ids=true | all-gather | bytes 6400 | tf_op jit(solution)/shard_map/all_gather | solution.py:101
  564.2 3.0 convolution_reduce_fusion
  (442 shorter events, 175.0 us)
Async XLA Ops:
  7.2 505.0 %copy-start = (bf16[640,2560]{1,0:T(8,128)(2,1)S(1)}, bf16[640,2560]{1,0:T(8,128)(2,1)}, u32[]{:S(2)}) copy-start(bf16[640,2560]{1,0:T(8,128)(2,1)} %param.15) | copy-start | bytes 9830404
  7.2 277.9 %all-gather.8.cloned.1.call-start = ((), (), s32[]{:S(2)}) async-start(), calls=%async_computation.1 | async-start | bytes 10649600 | tf_op jit(solution)/shard_map/all_gather | solution.py:10
  196.1 344.0 %reduce-scatter.4.cloned.1.call-start = ((), (), s32[]{:S(2)}) async-start(), calls=%async_computation.2 | async-start | bytes 1638400
  239.6 0.7 copy-start.1
  283.6 0.7 copy-start.2
  512.0 29.1 %copy-start.3 = (bf16[1,640]{1,0:T(2,128)(2,1)S(1)}, bf16[1,640]{1,0:T(2,128)(2,1)}, u32[]{:S(2)}) copy-start(bf16[1,640]{1,0:T(2,128)(2,1)} %param.14) | copy-start | bytes 3844
Sparse Core Ops, SparseCore 0:
  196.2 83.4 all-gather.7
  514.7 25.3 reduce-scatter.3
where the time goes:
time: 583 us; the launch traced here: 575 us
  local copies, waits for them, and re-layouts  207 us (36%)
  other arithmetic  158 us (27%)
  blocking collectives  153 us (26%)
  waiting for transfers between devices  24.8 us (4%)
  between operations  14.9 us (3%)
  matrix products  14.6 us (3%)
    add x63, other arithmetic, combine_parts(): total = scale_a * total_a + scale_b * total_b  86.1 us
    all_gather x2, blocking collectives, joined(): gathered = jax.tree.map(lambda a: lax.all_gather(a, axis), part)  85 us
    add x63, other arithmetic, combine_parts(): out_a.reshape(shape[:-1] + (group, -1)) * scale_a[..., None]  66.1 us
    scatter x1, local copies, waits for them, and re-layouts, per_device(): jnp.full((num_blocks,), -1, jnp.int32).at[target].set(req_ids, mode='drop')  60.5 us
    scatter x1, local copies, waits for them, and re-layouts, per_device(): jnp.zeros((num_blocks,), jnp.int32).at[target].set(slot_ids, mode='drop')  60.5 us
    dynamic_slice x192, local copies, waits for them, and re-layouts, take(): lax.dynamic_index_in_dim(a, source, 0, False)  56.8 us
    all_gather x1, blocking collectives, per_device(): every_query = lax.all_gather(queries, 'blk', axis=0, tiled=True)  46.6 us
    unnamed x3, waiting for transfers between devices  24.8 us
  transfers between devices with their start and end apart: 2, of which 1 were waited for; matrix products, arithmetic and copies ran while one was open for 1% of the time, Pallas kernels for 0%

commit v1 on v0

v1 whole, which is shorter than its diff:
```python
import functools

import jax
import jax.numpy as jnp
from jax import lax
from jax.experimental import pallas as pl
from jax.experimental.pallas import tpu as pltpu
from jax.sharding import PartitionSpec as P

HEAD = 128
MESH = pl.DeviceIdType.MESH
F32 = jnp.float32
BF16 = jnp.bfloat16
NEG = -1e30


def rows_of(x, count, width):
    rows = [x[:, i * width : (i + 1) * width] for i in range(count)]
    rows.append(jnp.zeros((8 - count, width), x.dtype))
    return jnp.concatenate(rows, axis=0)


def split(x):
    hi = x.astype(BF16)
    return hi, (x - hi.astype(F32)).astype(BF16)


def dot(a, b):
    return jnp.dot(a, b, preferred_element_type=F32)


def kernel(
    num_blk, num_kv, group,
    q_hbm, kv_hbm, table_hbm, len_hbm, res_hbm, wo_hbm, gain_hbm, wq_hbm,
    stream_ref, next_ref,
    q_v, kv_v, table_v, len_s, res_v, wo_v, gain_v, wq_v,
    qsend, qall, code_v, expand, count8, qblk, outs, msgf, msg, recv, recvf, hbuf, hsum,
    local_sem, qs_sem, qr_sem, ms_sem, mr_sem, hs_sem, hr_sem,
):
    me = lax.axis_index("blk")
    kv = lax.axis_index("kv")
    num_req = qall.shape[0]
    blocks = kv_v.shape[0]
    block = kv_v.shape[2]
    width = hsum.shape[1]
    cols = res_v.shape[1]

    pairs = [
        (q_hbm, q_v), (table_hbm, table_v), (len_hbm, len_s), (kv_hbm, kv_v),
        (res_hbm, res_v), (gain_hbm, gain_v), (wo_hbm, wo_v), (wq_hbm, wq_v),
    ]
    loads = [pltpu.make_async_copy(a, b, local_sem.at[i]) for i, (a, b) in enumerate(pairs)]

    def peer_of(j):
        step = num_blk // 2 + (1 - 2 * (j % 2)) * ((j + 1) // 2)
        return lax.rem(me + step, num_blk)

    barrier = pltpu.get_barrier_semaphore()
    loads[0].start()
    loads[1].start()
    loads[2].start()

    def greet(j, carry):
        pl.semaphore_signal(barrier, inc=1, device_id={"blk": peer_of(j)}, device_id_type=MESH)
        return carry

    lax.fori_loop(0, num_blk - 1, greet, 0)
    for j in range(1, num_kv):
        pl.semaphore_signal(
            barrier, inc=1, device_id={"kv": lax.rem(kv + j, num_kv)}, device_id_type=MESH
        )
    for load in loads[3:]:
        load.start()

    loads[0].wait()
    mine = rows_of(q_v[...].astype(F32), group, HEAD).astype(BF16)
    qsend[...] = mine
    qall[me] = mine

    loads[1].wait()
    loads[2].wait()
    max_blocks = table_v.shape[1]
    lane = lax.broadcasted_iota(jnp.int32, (1, 128), 1)
    row_id = lax.broadcasted_iota(jnp.int32, (blocks, 128), 0)
    best = jnp.full((blocks, 128), -1.0, F32)
    first = me * blocks
    for part in range(max_blocks // 128):
        at = lane + part * 128

        def match(i, acc):
            local = table_v[pl.ds(pl.multiple_of(i * 8, 8), 8), part * 128 : (part + 1) * 128] - first
            for c in range(8):
                r = i * 8 + c
                tokens = jnp.clip(len_s[r] - at * block, 0, block)
                code = (tokens + r * 128).astype(F32)
                acc = jnp.where(row_id == local[c : c + 1, :], code, acc)
            return acc

        best = lax.fori_loop(0, num_req // 8, match, best)
    code = jnp.broadcast_to(jnp.max(best, axis=1, keepdims=True), (blocks, 128))
    code_v[...] = code
    code_row = jnp.transpose(code)[:num_req, :].astype(jnp.int32)
    owns = (code_row >> 7) == lax.broadcasted_iota(jnp.int32, (num_req, blocks), 0)

    column = lax.broadcasted_iota(jnp.int32, (16, num_req * 8), 1)
    sub = lax.broadcasted_iota(jnp.int32, (16, 128), 0)

    def widen(i, carry):
        a = jnp.broadcast_to(code_v[pl.ds(2 * i, 1), :], (16, 128))
        b = jnp.broadcast_to(code_v[pl.ds(2 * i + 1, 1), :], (16, 128))
        both = jnp.where(sub < 8, a, b).astype(jnp.int32)
        target = (both >> 7) * 8 + (sub & 7)
        wide = jnp.concatenate([target] * (num_req * 8 // 128), axis=1)
        at16 = pl.multiple_of(i * 16, 16)
        expand[pl.ds(at16, 16), :] = jnp.where(column == wide, 1.0, 0.0).astype(BF16)
        count8[pl.ds(at16, 16), :] = jnp.where(both >= 0, both & 127, 0)
        return carry

    lax.fori_loop(0, blocks // 2, widen, 0, unroll=4)

    pl.semaphore_wait(barrier, num_blk - 1 + num_kv - 1)

    def send_query(j, carry):
        pltpu.make_async_remote_copy(
            src_ref=qsend, dst_ref=qall.at[me], send_sem=qs_sem, recv_sem=qr_sem,
            device_id={"blk": peer_of(j)}, device_id_type=MESH,
        ).start()
        return carry

    lax.fori_loop(0, num_blk - 1, send_query, 0)
    loads[3].wait()
    others = pl.ds(0, num_blk - 1)
    pltpu.make_async_copy(qall.at[others], qall.at[others], qr_sem).wait()

    flat = qall[...].astype(F32).reshape(num_req * 8, HEAD).astype(BF16)
    qblk[...] = dot(expand[...], flat).astype(BF16)

    rows = 32
    toks = 4 * block
    r_i = lax.broadcasted_iota(jnp.int32, (rows, toks), 0) // 8
    t_i = lax.broadcasted_iota(jnp.int32, (rows, toks), 1)
    token = jnp.where(t_i // block == r_i, t_i % block, 4096)
    lane8 = lax.broadcasted_iota(jnp.int32, (8, 128), 1)
    scale = HEAD ** (-0.5)

    def attend(i, carry):
        bmax, bsum = carry
        for u in range(4):
            g = i * 4 + u
            at = pl.multiple_of(g * rows, rows)
            q = qblk[pl.ds(at, rows), :]
            k = kv_v[pl.ds(g * 4, 4), 0].reshape(toks, HEAD)
            v = kv_v[pl.ds(g * 4, 4), 1].reshape(toks, HEAD)
            s = lax.dot_general(q, k, (((1,), (1,)), ((), ())), preferred_element_type=F32) * scale
            n = count8[pl.ds(at, rows), :]
            ok = token < jnp.concatenate([n] * (toks // 128), axis=1)
            s = jnp.where(ok, s, NEG)
            m = jnp.max(s, axis=1, keepdims=True)
            e = jnp.where(ok, jnp.exp(s - m), 0.0)
            l = jnp.sum(e, axis=1, keepdims=True)
            outs[pl.ds(at, rows), :] = dot(e.astype(BF16), v)
            for c in range(4):
                here = lane8 == g * 4 + c
                bmax = jnp.where(here, m[c * 8 : (c + 1) * 8], bmax)
                bsum = jnp.where(here, l[c * 8 : (c + 1) * 8], bsum)
        return bmax, bsum

    zero8 = jnp.zeros((8, 128), F32)
    bmax, bsum = lax.fori_loop(0, blocks // 16, attend, (zero8, zero8))

    lane_r = lax.broadcasted_iota(jnp.int32, (num_req, 128), 1)
    tops = jnp.zeros((num_req, 128), F32)
    sums = jnp.zeros((num_req, 128), F32)
    for h in range(group):
        high = jnp.where(owns, bmax[h : h + 1, :], NEG)
        top = jnp.max(high, axis=1, keepdims=True).astype(BF16).astype(F32)
        w = jnp.where(owns, jnp.exp(high - top), 0.0)
        total = jnp.sum(w * bsum[h : h + 1, :], axis=1, keepdims=True)
        w_hi, w_lo = split(w)
        o_hi, o_lo = split(outs[pl.ds(h, blocks, stride=8), :])
        acc = dot(w_hi, o_hi) + dot(w_hi, o_lo) + dot(w_lo, o_hi)
        msgf[pl.ds(h, num_req, stride=8), :] = acc
        tops = jnp.where(lane_r == h, top, tops)
        sums = jnp.where(lane_r == h, total, sums)
    sum_hi = sums.astype(BF16).astype(F32)
    msgf[pl.ds(group, num_req, stride=8), :] = tops
    msgf[pl.ds(group + 1, num_req, stride=8), :] = sum_hi
    msgf[pl.ds(group + 2, num_req, stride=8), :] = sums - sum_hi
    msg[...] = msgf[...].reshape(num_req, 8, 128).astype(BF16)
    recv[me] = msg[me]

    def send_part(j, carry):
        peer = peer_of(j)
        pltpu.make_async_remote_copy(
            src_ref=msg.at[peer], dst_ref=recv.at[me], send_sem=ms_sem, recv_sem=mr_sem,
            device_id={"blk": peer}, device_id_type=MESH,
        ).start()
        return carry

    lax.fori_loop(0, num_blk - 1, send_part, 0)
    for load in loads[4:]:
        load.wait()
    pltpu.make_async_copy(recv.at[others], recv.at[others], mr_sem).wait()

    recvf[...] = recv[...].astype(F32).reshape(num_blk * 8, 128)
    tops = recvf[pl.ds(group, num_blk, stride=8), :]
    sums = recvf[pl.ds(group + 1, num_blk, stride=8), :] + recvf[pl.ds(group + 2, num_blk, stride=8), :]
    w = jnp.exp(tops - jnp.max(tops, axis=0, keepdims=True))
    total = jnp.sum(w * sums, axis=0, keepdims=True)
    heads = []
    for h in range(group):
        acc = jnp.sum(w[:, h : h + 1] * recvf[pl.ds(h, num_blk, stride=8), :], axis=0, keepdims=True)
        heads.append(acc / total[:, h : h + 1])
    attn = jnp.concatenate(heads, axis=1)
    attn8 = jnp.broadcast_to(attn, (8, group * HEAD)).astype(BF16)
    hbuf[kv] = dot(attn8, wo_v[...])[:1, :]
    own = pl.ds(pl.multiple_of(kv * cols, 128), cols)
    hbuf[kv, :, own] = hbuf[kv, :, own] + res_v[...].astype(F32)

    hops = []
    for j in range(1, num_kv):
        hops.append(pltpu.make_async_remote_copy(
            src_ref=hbuf.at[kv], dst_ref=hbuf.at[kv], send_sem=hs_sem.at[j - 1], recv_sem=hr_sem.at[j - 1],
            device_id={"kv": lax.rem(kv + j, num_kv)}, device_id_type=MESH,
        ))
    for hop in hops:
        hop.start()
    for hop in hops:
        hop.wait_recv()

    hidden = hbuf[0]
    for j in range(1, num_kv):
        hidden = hidden + hbuf[j]
    hsum[...] = hidden
    inverse = lax.rsqrt(jnp.sum(hidden * hidden, axis=1, keepdims=True) / width + 1e-05)
    normed = hidden * inverse * gain_v[...].astype(F32)
    normed8 = jnp.broadcast_to(normed, (8, width)).astype(BF16)
    next_ref[...] = dot(normed8, wq_v[...])[:1, :].astype(BF16)
    stream_ref[...] = hsum[:, own].astype(BF16)

    for hop in hops:
        hop.wait_send()
    pltpu.make_async_copy(qall.at[others], qall.at[others], qs_sem).wait()
    pltpu.make_async_copy(recv.at[others], recv.at[others], ms_sem).wait()


def per_device(num_blk, num_kv, queries, kv_pool, block_table, lengths, residual, out_weight, norm_gain, qkv_weight):
    group = queries.shape[1] // HEAD
    num_req, max_blocks = block_table.shape
    blocks, _, block, _ = kv_pool.shape
    width = out_weight.shape[1]
    cols = residual.shape[1]
    out_cols = qkv_weight.shape[1]
    anywhere = pl.BlockSpec(memory_space=pl.ANY)
    vmem = pl.BlockSpec(memory_space=pltpu.VMEM)
    dma = pltpu.SemaphoreType.DMA
    return pl.pallas_call(
        functools.partial(kernel, num_blk, num_kv, group),
        out_shape=(
            jax.ShapeDtypeStruct((1, cols), BF16),
            jax.ShapeDtypeStruct((1, out_cols), BF16),
        ),
        in_specs=[anywhere] * 8,
        out_specs=(vmem, vmem),
        scratch_shapes=[
            pltpu.VMEM(queries.shape, BF16),
            pltpu.VMEM(kv_pool.shape, BF16),
            pltpu.VMEM(block_table.shape, jnp.int32),
            pltpu.SMEM((num_req,), jnp.int32),
            pltpu.VMEM(residual.shape, BF16),
            pltpu.VMEM(out_weight.shape, BF16),
            pltpu.VMEM((1, width), BF16),
            pltpu.VMEM(qkv_weight.shape, BF16),
            pltpu.VMEM((8, HEAD), BF16),
            pltpu.VMEM((num_req, 8, HEAD), BF16),
            pltpu.VMEM((blocks, 128), F32),
            pltpu.VMEM((blocks * 8, num_req * 8), BF16),
            pltpu.VMEM((blocks * 8, 128), jnp.int32),
            pltpu.VMEM((blocks * 8, HEAD), BF16),
            pltpu.VMEM((blocks * 8, HEAD), F32),
            pltpu.VMEM((num_req * 8, HEAD), F32),
            pltpu.VMEM((num_req, 8, HEAD), BF16),
            pltpu.VMEM((num_blk, 8, HEAD), BF16),
            pltpu.VMEM((num_blk * 8, HEAD), F32),
            pltpu.VMEM((num_kv, 1, width), F32),
            pltpu.VMEM((1, width), F32),
            dma((8,)), dma, dma, dma, dma, dma((num_kv - 1,)), dma((num_kv - 1,)),
        ],
        compiler_params=pltpu.CompilerParams(
            collective_id=0, has_side_effects=True, vmem_limit_bytes=60 * 1024 * 1024
        ),
    )(queries, kv_pool, block_table, lengths, residual, out_weight, norm_gain.reshape(1, -1), qkv_weight)


def solution(mesh):
    placed = (
        P("blk", "kv"),
        P("blk", None, None, "kv"),
        P(),
        P(),
        P("blk", "kv"),
        P("kv", None),
        P(),
        P(None, "kv"),
    )
    return jax.shard_map(
        functools.partial(per_device, mesh.shape["blk"], mesh.shape["kv"]),
        mesh=mesh,
        in_specs=placed,
        out_specs=(P("blk", "kv"), P("blk", "kv")),
        check_vma=False,
    )
```

time: 583 us -> 44.8 us (0.08)
  the two profiles are of different devices: /device:TPU:2 before, /device:TPU:1 now
where the time goes in v1:
time: 44.8 us; the launch traced here: 44.6 us
  Pallas kernels  40.2 us (90%)
  local copies, waits for them, and re-layouts  3.78 us (8%)
  between operations  0.64 us (1%)
    pallas_call x1, Pallas kernels, per_device(): pl.pallas_call(functools.partial(kernel, num_blk, num_kv, group), out_sha...  40.2 us
    unnamed x2, local copies, waits for them, and re-layouts  2.49 us
    reshape x1, local copies, waits for them, and re-layouts, per_device(): norm_gain.reshape(1, -1)  1.29 us

profile of v1, /device:TPU:1, one launch (start us, length us, event | category | flops | bytes accessed | tf_op | source)
XLA Modules:
  0.0 44.6 jit_solution(6194491460770963186)
XLA Ops:
  0.6 1.3 %reshape.7.gain_hbm = bf16[1,2560]{1,0:T(2,128)(2,1)} reshape(bf16[2560]{0:T(1024)(128)(2,1)} %param.14) | data formatting | bytes 10240 | tf_op jit(solution)/shard_map/reshape | solution.py:292
  1.9 40.2 %shard_map.95 = (bf16[1,640]{1,0:T(2,128)(2,1)}, bf16[1,896]{1,0:T(2,128)(2,1)}) custom-call(bf16[1,640]{1,0:T(2,128)(2,1)} %q_hbm.1, bf16[128,2,64,128]{3,2,1,0:T(8,128)(2,1)} %kv_hbm.1, s32[64,256]{1,0:T(8,128)} %table_hbm.1, s32[64]{0:T(128)} %len_hbm.1, bf16[1,640]{1,0:T(2,128)(2,1)} %res_hbm.1, bf16[640,2560]{1,0:T(8,128)(2,1)} %wo_hbm.1, ...), custom_call_target="tpu_custom_call" | custom-call | tf_op jit(solution)/shard_map/pallas_call | solution.py:257
  42.1 1.2 %copy.12 = bf16[1,640]{1,0:T(2,128)(2,1)} copy(bf16[1,640]{1,0:T(2,128)(2,1)} %get-tuple-element.4) | data formatting | bytes 2560
  43.4 1.2 %copy.13 = bf16[1,896]{1,0:T(2,128)(2,1)} copy(bf16[1,896]{1,0:T(2,128)(2,1)} %get-tuple-element.5) | data formatting | bytes 3584

commit v2 on v1

--- a/solution.py
+++ b/solution.py
@@ -12,6 +12,7 @@
 F32 = jnp.float32
 BF16 = jnp.bfloat16
 NEG = -1e30
+INNER = 8
 
 
 def rows_of(x, count, width):
@@ -30,14 +31,18 @@
 
 
 def kernel(
-    num_blk, num_kv, group,
+    num_blk, inner, num_kv, group,
     q_hbm, kv_hbm, table_hbm, len_hbm, res_hbm, wo_hbm, gain_hbm, wq_hbm,
     stream_ref, next_ref,
     q_v, kv_v, table_v, len_s, res_v, wo_v, gain_v, wq_v,
-    qsend, qall, code_v, expand, count8, qblk, outs, msgf, msg, recv, recvf, hbuf, hsum,
+    qall, code_v, expand, count8, qblk, outs, msgf, msg, recv, recvf, hbuf, hsum,
     local_sem, qs_sem, qr_sem, ms_sem, mr_sem, hs_sem, hr_sem,
 ):
     me = lax.axis_index("blk")
+    num_ring = num_blk // inner
+    ring = me // inner
+    spot = lax.rem(me, inner)
+    near = sorted(range(1, num_ring), key=lambda k: min(k, num_ring - k))
     kv = lax.axis_index("kv")
     num_req = qall.shape[0]
     blocks = kv_v.shape[0]
@@ -60,21 +65,25 @@
     loads[1].start()
     loads[2].start()
 
-    def greet(j, carry):
-        pl.semaphore_signal(barrier, inc=1, device_id={"blk": peer_of(j)}, device_id_type=MESH)
-        return carry
-
-    lax.fori_loop(0, num_blk - 1, greet, 0)
-    for j in range(1, num_kv):
+    def along(k):
+        return {"blk": lax.rem(ring + k, num_ring) * inner + spot}
+
+    def across(k):
+        return {"blk": ring * inner + lax.rem(spot + k, inner)}
+
+    for k in near:
+        pl.semaphore_signal(barrier, inc=1, device_id=along(k), device_id_type=MESH)
+    for k in range(1, inner):
+        pl.semaphore_signal(barrier, inc=1, device_id=across(k), device_id_type=MESH)
+    for k in range(1, num_kv):
         pl.semaphore_signal(
-            barrier, inc=1, device_id={"kv": lax.rem(kv + j, num_kv)}, device_id_type=MESH
+            barrier, inc=1, device_id={"kv": lax.rem(kv + k, num_kv)}, device_id_type=MESH
         )
     for load in loads[3:]:
         load.start()
 
     loads[0].wait()
     mine = rows_of(q_v[...].astype(F32), group, HEAD).astype(BF16)
-    qsend[...] = mine
     qall[me] = mine
 
     loads[1].wait()
@@ -118,19 +127,28 @@
 
     lax.fori_loop(0, blocks // 2, widen, 0, unroll=4)
 
-    pl.semaphore_wait(barrier, num_blk - 1 + num_kv - 1)
-
-    def send_query(j, carry):
-        pltpu.make_async_remote_copy(
-            src_ref=qsend, dst_ref=qall.at[me], send_sem=qs_sem, recv_sem=qr_sem,
-            device_id={"blk": peer_of(j)}, device_id_type=MESH,
-        ).start()
-        return carry
-
-    lax.fori_loop(0, num_blk - 1, send_query, 0)
+    pl.semaphore_wait(barrier, num_ring - 1 + inner - 1 + num_kv - 1)
+
+    def query(slot, k, device, send, arrive):
+        return pltpu.make_async_remote_copy(
+            src_ref=qall.at[slot], dst_ref=qall.at[slot], send_sem=send, recv_sem=arrive,
+            device_id=device, device_id_type=MESH,
+        )
+
+    ahead = [query(me, k, along(k), qs_sem.at[k], qr_sem.at[k]) for k in near]
+    for copy in ahead[::-1]:
+        copy.start()
+    for k in range(1, inner):
+        query(me, k, across(k), qs_sem.at[0], qr_sem.at[0]).start()
+    for k, copy in zip(near, ahead):
+        copy.wait_recv()
+        source = lax.rem(ring + num_ring - k, num_ring) * inner + spot
+        for c in range(1, inner):
+            query(source, c, across(c), qs_sem.at[0], qr_sem.at[0]).start()
     loads[3].wait()
     others = pl.ds(0, num_blk - 1)
-    pltpu.make_async_copy(qall.at[others], qall.at[others], qr_sem).wait()
+    passed = pl.ds(0, (inner - 1) * num_ring)
+    pltpu.make_async_copy(qall.at[passed], qall.at[passed], qr_sem.at[0]).wait()
 
     flat = qall[...].astype(F32).reshape(num_req * 8, HEAD).astype(BF16)
     qblk[...] = dot(expand[...], flat).astype(BF16)
@@ -142,31 +160,30 @@
     token = jnp.where(t_i // block == r_i, t_i % block, 4096)
     lane8 = lax.broadcasted_iota(jnp.int32, (8, 128), 1)
     scale = HEAD ** (-0.5)
-
-    def attend(i, carry):
-        bmax, bsum = carry
-        for u in range(4):
-            g = i * 4 + u
-            at = pl.multiple_of(g * rows, rows)
-            q = qblk[pl.ds(at, rows), :]
-            k = kv_v[pl.ds(g * 4, 4), 0].reshape(toks, HEAD)
-            v = kv_v[pl.ds(g * 4, 4), 1].reshape(toks, HEAD)
-            s = lax.dot_general(q, k, (((1,), (1,)), ((), ())), preferred_element_type=F32) * scale
-            n = count8[pl.ds(at, rows), :]
-            ok = token < jnp.concatenate([n] * (toks // 128), axis=1)
-            s = jnp.where(ok, s, NEG)
-            m = jnp.max(s, axis=1, keepdims=True)
-            e = jnp.where(ok, jnp.exp(s - m), 0.0)
-            l = jnp.sum(e, axis=1, keepdims=True)
-            outs[pl.ds(at, rows), :] = dot(e.astype(BF16), v)
-            for c in range(4):
-                here = lane8 == g * 4 + c
-                bmax = jnp.where(here, m[c * 8 : (c + 1) * 8], bmax)
-                bsum = jnp.where(here, l[c * 8 : (c + 1) * 8], bsum)
-        return bmax, bsum
-
-    zero8 = jnp.zeros((8, 128), F32)
-    bmax, bsum = lax.fori_loop(0, blocks // 16, attend, (zero8, zero8))
+    groups = blocks // 4
+    scores = []
+    for g in range(groups):
+        q = qblk[g * rows : (g + 1) * rows, :]
+        k = kv_v[g * 4 : (g + 1) * 4, 0].reshape(toks, HEAD)
+        scores.append(lax.dot_general(q, k, (((1,), (1,)), ((), ())), preferred_element_type=F32))
+    bmax = jnp.zeros((8, 128), F32)
+    bsum = jnp.zeros((8, 128), F32)
+    weights = []
+    for g in range(groups):
+        n = count8[g * rows : (g + 1) * rows, :]
+        ok = token < jnp.concatenate([n] * (toks // 128), axis=1)
+        s = jnp.where(ok, scores[g] * scale, NEG)
+        m = jnp.max(s, axis=1, keepdims=True)
+        e = jnp.exp(s - m)
+        l = jnp.sum(e, axis=1, keepdims=True)
+        weights.append(e.astype(BF16))
+        for c in range(4):
+            here = lane8 == g * 4 + c
+            bmax = jnp.where(here, m[c * 8 : (c + 1) * 8], bmax)
+            bsum = jnp.where(here, l[c * 8 : (c + 1) * 8], bsum)
+    for g in range(groups):
+        v = kv_v[g * 4 : (g + 1) * 4, 1].reshape(toks, HEAD)
+        outs[g * rows : (g + 1) * rows, :] = dot(weights[g], v)
 
     lane_r = lax.broadcasted_iota(jnp.int32, (num_req, 128), 1)
     tops = jnp.zeros((num_req, 128), F32)
@@ -202,6 +219,8 @@
         load.wait()
     pltpu.make_async_copy(recv.at[others], recv.at[others], mr_sem).wait()
 
+    gain = gain_v[...].astype(F32)
+    gain = jnp.concatenate([gain[i : i + 1, :] for i in range(width // 128)], axis=1)
     recvf[...] = recv[...].astype(F32).reshape(num_blk * 8, 128)
     tops = recvf[pl.ds(group, num_blk, stride=8), :]
     sums = recvf[pl.ds(group + 1, num_blk, stride=8), :] + recvf[pl.ds(group + 2, num_blk, stride=8), :]
@@ -233,18 +252,20 @@
         hidden = hidden + hbuf[j]
     hsum[...] = hidden
     inverse = lax.rsqrt(jnp.sum(hidden * hidden, axis=1, keepdims=True) / width + 1e-05)
-    normed = hidden * inverse * gain_v[...].astype(F32)
+    normed = hidden * inverse * gain
     normed8 = jnp.broadcast_to(normed, (8, width)).astype(BF16)
     next_ref[...] = dot(normed8, wq_v[...])[:1, :].astype(BF16)
     stream_ref[...] = hsum[:, own].astype(BF16)
 
     for hop in hops:
         hop.wait_send()
-    pltpu.make_async_copy(qall.at[others], qall.at[others], qs_sem).wait()
+    for copy in ahead:
+        copy.wait_send()
+    pltpu.make_async_copy(qall.at[passed], qall.at[passed], qs_sem.at[0]).wait()
     pltpu.make_async_copy(recv.at[others], recv.at[others], ms_sem).wait()
 
 
-def per_device(num_blk, num_kv, queries, kv_pool, block_table, lengths, residual, out_weight, norm_gain, qkv_weight):
+def per_device(num_blk, inner, num_kv, queries, kv_pool, block_table, lengths, residual, out_weight, norm_gain, qkv_weight):
     group = queries.shape[1] // HEAD
     num_req, max_blocks = block_table.shape
     blocks, _, block, _ = kv_pool.shape
@@ -255,7 +276,7 @@
     vmem = pl.BlockSpec(memory_space=pltpu.VMEM)
     dma = pltpu.SemaphoreType.DMA
     return pl.pallas_call(
-        functools.partial(kernel, num_blk, num_kv, group),
+        functools.partial(kernel, num_blk, inner, num_kv, group),
         out_shape=(
             jax.ShapeDtypeStruct((1, cols), BF16),
             jax.ShapeDtypeStruct((1, out_cols), BF16),
@@ -269,9 +290,8 @@
             pltpu.SMEM((num_req,), jnp.int32),
             pltpu.VMEM(residual.shape, BF16),
             pltpu.VMEM(out_weight.shape, BF16),
-            pltpu.VMEM((1, width), BF16),
+            pltpu.VMEM((width // 128, 128), BF16),
             pltpu.VMEM(qkv_weight.shape, BF16),
-            pltpu.VMEM((8, HEAD), BF16),
             pltpu.VMEM((num_req, 8, HEAD), BF16),
             pltpu.VMEM((blocks, 128), F32),
             pltpu.VMEM((blocks * 8, num_req * 8), BF16),
@@ -284,12 +304,12 @@
             pltpu.VMEM((num_blk * 8, HEAD), F32),
             pltpu.VMEM((num_kv, 1, width), F32),
             pltpu.VMEM((1, width), F32),
-            dma((8,)), dma, dma, dma, dma, dma((num_kv - 1,)), dma((num_kv - 1,)),
+            dma((8,)), dma((num_blk // inner,)), dma((num_blk // inner,)), dma, dma, dma((num_kv - 1,)), dma((num_kv - 1,)),
         ],
         compiler_params=pltpu.CompilerParams(
             collective_id=0, has_side_effects=True, vmem_limit_bytes=60 * 1024 * 1024
         ),
-    )(queries, kv_pool, block_table, lengths, residual, out_weight, norm_gain.reshape(1, -1), qkv_weight)
+    )(queries, kv_pool, block_table, lengths, residual, out_weight, norm_gain.reshape(-1, 128), qkv_weight)
 
 
 def solution(mesh):
@@ -304,7 +324,7 @@
         P(None, "kv"),
     )
     return jax.shard_map(
-        functools.partial(per_device, mesh.shape["blk"], mesh.shape["kv"]),
+        functools.partial(per_device, mesh.shape["blk"], INNER, mesh.shape["kv"]),
         mesh=mesh,
         in_specs=placed,
         out_specs=(P("blk", "kv"), P("blk", "kv")),

time: 44.8 us -> 35.8 us (0.80)
  Pallas kernels: 40.2 us -> 32.5 us
  local copies, waits for them, and re-layouts: 3.78 us -> 2.49 us
    pallas_call x1, Pallas kernels: 40.2 us -> 32.5 us  [per_device(): pl.pallas_call(functools.partial(kernel, num_blk, inner, num_kv, group),...]
    reshape x1 -> x0, local copies, waits for them, and re-layouts: 1.29 us -> none  [per_device(): norm_gain.reshape(1, -1)]
where the time goes in v2:
time: 35.8 us; the launch traced here: 35.7 us
  Pallas kernels  32.5 us (91%)
  local copies, waits for them, and re-layouts  2.49 us (7%)
  between operations  0.64 us (2%)
    pallas_call x1, Pallas kernels, per_device(): pl.pallas_call(functools.partial(kernel, num_blk, inner, num_kv, group),...  32.5 us
    unnamed x2, local copies, waits for them, and re-layouts  2.49 us

profile of v2, /device:TPU:1, one launch (start us, length us, event | category | flops | bytes accessed | tf_op | source)
XLA Modules:
  0.0 35.7 jit_solution(2841067275819608233)
XLA Ops:
  0.6 32.5 %shard_map.95 = (bf16[1,640]{1,0:T(2,128)(2,1)}, bf16[1,896]{1,0:T(2,128)(2,1)}) custom-call(bf16[1,640]{1,0:T(2,128)(2,1)} %q_hbm.1, bf16[128,2,64,128]{3,2,1,0:T(8,128)(2,1)} %kv_hbm.1, s32[64,256]{1,0:T(8,128)} %table_hbm.1, s32[64]{0:T(128)} %len_hbm.1, bf16[1,640]{1,0:T(2,128)(2,1)} %res_hbm.1, bf16[640,2560]{1,0:T(8,128)(2,1)} %wo_hbm.1, ...), custom_call_target="tpu_custom_call" | custom-call | tf_op jit(solution)/shard_map/pallas_call | solution.py:278
  33.2 1.2 %copy.12 = bf16[1,640]{1,0:T(2,128)(2,1)} copy(bf16[1,640]{1,0:T(2,128)(2,1)} %get-tuple-element.4) | data formatting | bytes 2560
  34.4 1.3 %copy.13 = bf16[1,896]{1,0:T(2,128)(2,1)} copy(bf16[1,896]{1,0:T(2,128)(2,1)} %get-tuple-element.5) | data formatting | bytes 3584

commit v3 on v2

--- a/solution.py
+++ b/solution.py
@@ -12,7 +12,7 @@
 F32 = jnp.float32
 BF16 = jnp.bfloat16
 NEG = -1e30
-INNER = 8
+CHIPS_X = 4
 
 
 def rows_of(x, count, width):
@@ -31,19 +31,32 @@
 
 
 def kernel(
-    num_blk, inner, num_kv, group,
+    num_blk, num_x, num_kv, group,
     q_hbm, kv_hbm, table_hbm, len_hbm, res_hbm, wo_hbm, gain_hbm, wq_hbm,
-    stream_ref, next_ref,
+    both_ref,
     q_v, kv_v, table_v, len_s, res_v, wo_v, gain_v, wq_v,
     qall, code_v, expand, count8, qblk, outs, msgf, msg, recv, recvf, hbuf, hsum,
-    local_sem, qs_sem, qr_sem, ms_sem, mr_sem, hs_sem, hr_sem,
+    local_sem, ready, qs_sem, qr_sem, ms_sem, mr_sem, hs_sem, hr_sem,
 ):
     me = lax.axis_index("blk")
-    num_ring = num_blk // inner
-    ring = me // inner
-    spot = lax.rem(me, inner)
-    near = sorted(range(1, num_ring), key=lambda k: min(k, num_ring - k))
     kv = lax.axis_index("kv")
+    num_z = num_blk // (num_x * 2)
+    core = lax.rem(me, 2)
+    x_at = [lax.rem(me // 2 + k, num_x) * 2 for k in range(num_x)]
+    z_at = [lax.rem(me // (num_x * 2) + k, num_z) * (num_x * 2) for k in range(num_z)]
+    core_at = [core, 1 - core]
+
+    def peer(k):
+        return z_at[k[0]] + x_at[k[1]] + core_at[k[2]]
+
+    def hops(k):
+        return min(k[0], num_z - k[0]) + min(k[1], num_x - k[1]) + 0.1 * k[2]
+
+    others = [(a, b, c) for a in range(num_z) for b in range(num_x) for c in range(2)][1:]
+    others.sort(key=hops, reverse=True)
+    plane = [k for k in others if k[0] == 0]
+    column = [k for k in others if k[1:] == (0, 0)]
+    rest = [k for k in others if k not in plane and k not in column]
     num_req = qall.shape[0]
     blocks = kv_v.shape[0]
     block = kv_v.shape[2]
@@ -56,25 +69,13 @@
     ]
     loads = [pltpu.make_async_copy(a, b, local_sem.at[i]) for i, (a, b) in enumerate(pairs)]
 
-    def peer_of(j):
-        step = num_blk // 2 + (1 - 2 * (j % 2)) * ((j + 1) // 2)
-        return lax.rem(me + step, num_blk)
-
     barrier = pltpu.get_barrier_semaphore()
     loads[0].start()
     loads[1].start()
     loads[2].start()
 
-    def along(k):
-        return {"blk": lax.rem(ring + k, num_ring) * inner + spot}
-
-    def across(k):
-        return {"blk": ring * inner + lax.rem(spot + k, inner)}
-
-    for k in near:
-        pl.semaphore_signal(barrier, inc=1, device_id=along(k), device_id_type=MESH)
-    for k in range(1, inner):
-        pl.semaphore_signal(barrier, inc=1, device_id=across(k), device_id_type=MESH)
+    for k in column + plane:
+        pl.semaphore_signal(barrier, inc=1, device_id={"blk": peer(k)}, device_id_type=MESH)
     for k in range(1, num_kv):
         pl.semaphore_signal(
             barrier, inc=1, device_id={"kv": lax.rem(kv + k, num_kv)}, device_id_type=MESH
@@ -111,7 +112,7 @@
     code_row = jnp.transpose(code)[:num_req, :].astype(jnp.int32)
     owns = (code_row >> 7) == lax.broadcasted_iota(jnp.int32, (num_req, blocks), 0)
 
-    column = lax.broadcasted_iota(jnp.int32, (16, num_req * 8), 1)
+    col_id = lax.broadcasted_iota(jnp.int32, (16, num_req * 8), 1)
     sub = lax.broadcasted_iota(jnp.int32, (16, 128), 0)
 
     def widen(i, carry):
@@ -121,34 +122,31 @@
         target = (both >> 7) * 8 + (sub & 7)
         wide = jnp.concatenate([target] * (num_req * 8 // 128), axis=1)
         at16 = pl.multiple_of(i * 16, 16)
-        expand[pl.ds(at16, 16), :] = jnp.where(column == wide, 1.0, 0.0).astype(BF16)
+        expand[pl.ds(at16, 16), :] = jnp.where(col_id == wide, 1.0, 0.0).astype(BF16)
         count8[pl.ds(at16, 16), :] = jnp.where(both >= 0, both & 127, 0)
         return carry
 
     lax.fori_loop(0, blocks // 2, widen, 0, unroll=4)
 
-    pl.semaphore_wait(barrier, num_ring - 1 + inner - 1 + num_kv - 1)
-
-    def query(slot, k, device, send, arrive):
-        return pltpu.make_async_remote_copy(
-            src_ref=qall.at[slot], dst_ref=qall.at[slot], send_sem=send, recv_sem=arrive,
-            device_id=device, device_id_type=MESH,
-        )
-
-    ahead = [query(me, k, along(k), qs_sem.at[k], qr_sem.at[k]) for k in near]
-    for copy in ahead[::-1]:
-        copy.start()
-    for k in range(1, inner):
-        query(me, k, across(k), qs_sem.at[0], qr_sem.at[0]).start()
-    for k, copy in zip(near, ahead):
-        copy.wait_recv()
-        source = lax.rem(ring + num_ring - k, num_ring) * inner + spot
-        for c in range(1, inner):
-            query(source, c, across(c), qs_sem.at[0], qr_sem.at[0]).start()
+    pl.semaphore_wait(barrier, len(column) + len(plane) + num_kv - 1)
+
+    for k in plane:
+        pl.semaphore_signal(ready, inc=1, device_id={"blk": peer(k)}, device_id_type=MESH)
+
+    def send_query(k):
+        pltpu.make_async_remote_copy(
+            src_ref=qall.at[me], dst_ref=qall.at[me], send_sem=qs_sem, recv_sem=qr_sem,
+            device_id={"blk": peer(k)}, device_id_type=MESH,
+        ).start()
+
+    for k in column + plane:
+        send_query(k)
+    pl.semaphore_wait(ready, len(plane))
+    for k in rest:
+        send_query(k)
     loads[3].wait()
-    others = pl.ds(0, num_blk - 1)
-    passed = pl.ds(0, (inner - 1) * num_ring)
-    pltpu.make_async_copy(qall.at[passed], qall.at[passed], qr_sem.at[0]).wait()
+    rows63 = pl.ds(0, num_blk - 1)
+    pltpu.make_async_copy(qall.at[rows63], qall.at[rows63], qr_sem).wait()
 
     flat = qall[...].astype(F32).reshape(num_req * 8, HEAD).astype(BF16)
     qblk[...] = dot(expand[...], flat).astype(BF16)
@@ -206,18 +204,15 @@
     msg[...] = msgf[...].reshape(num_req, 8, 128).astype(BF16)
     recv[me] = msg[me]
 
-    def send_part(j, carry):
-        peer = peer_of(j)
+    for k in others:
+        to = peer(k)
         pltpu.make_async_remote_copy(
-            src_ref=msg.at[peer], dst_ref=recv.at[me], send_sem=ms_sem, recv_sem=mr_sem,
-            device_id={"blk": peer}, device_id_type=MESH,
+            src_ref=msg.at[to], dst_ref=recv.at[me], send_sem=ms_sem, recv_sem=mr_sem,
+            device_id={"blk": to}, device_id_type=MESH,
         ).start()
-        return carry
-
-    lax.fori_loop(0, num_blk - 1, send_part, 0)
     for load in loads[4:]:
         load.wait()
-    pltpu.make_async_copy(recv.at[others], recv.at[others], mr_sem).wait()
+    pltpu.make_async_copy(recv.at[rows63], recv.at[rows63], mr_sem).wait()
 
     gain = gain_v[...].astype(F32)
     gain = jnp.concatenate([gain[i : i + 1, :] for i in range(width // 128)], axis=1)
@@ -236,15 +231,15 @@
     own = pl.ds(pl.multiple_of(kv * cols, 128), cols)
     hbuf[kv, :, own] = hbuf[kv, :, own] + res_v[...].astype(F32)
 
-    hops = []
+    hops_y = []
     for j in range(1, num_kv):
-        hops.append(pltpu.make_async_remote_copy(
+        hops_y.append(pltpu.make_async_remote_copy(
             src_ref=hbuf.at[kv], dst_ref=hbuf.at[kv], send_sem=hs_sem.at[j - 1], recv_sem=hr_sem.at[j - 1],
             device_id={"kv": lax.rem(kv + j, num_kv)}, device_id_type=MESH,
         ))
-    for hop in hops:
+    for hop in hops_y:
         hop.start()
-    for hop in hops:
+    for hop in hops_y:
         hop.wait_recv()
 
     hidden = hbuf[0]
@@ -254,18 +249,22 @@
     inverse = lax.rsqrt(jnp.sum(hidden * hidden, axis=1, keepdims=True) / width + 1e-05)
     normed = hidden * inverse * gain
     normed8 = jnp.broadcast_to(normed, (8, width)).astype(BF16)
-    next_ref[...] = dot(normed8, wq_v[...])[:1, :].astype(BF16)
-    stream_ref[...] = hsum[:, own].astype(BF16)
-
-    for hop in hops:
+    both_ref[:, :cols] = hsum[:, own].astype(BF16)
+    both_ref[:, cols:] = dot(normed8, wq_v[...])[:1, :].astype(BF16)
+
+    for hop in hops_y:
         hop.wait_send()
-    for copy in ahead:
-        copy.wait_send()
-    pltpu.make_async_copy(qall.at[passed], qall.at[passed], qs_sem.at[0]).wait()
-    pltpu.make_async_copy(recv.at[others], recv.at[others], ms_sem).wait()
-
-
-def per_device(num_blk, inner, num_kv, queries, kv_pool, block_table, lengths, residual, out_weight, norm_gain, qkv_weight):
+    pltpu.make_async_copy(qall.at[rows63], qall.at[rows63], qs_sem).wait()
+    pltpu.make_async_copy(recv.at[rows63], recv.at[rows63], ms_sem).wait()
+
+
+def part(both_ref, stream_ref, next_ref):
+    cols = stream_ref.shape[1]
+    stream_ref[...] = both_ref[:, :cols]
+    next_ref[...] = both_ref[:, cols:]
+
+
+def per_device(num_blk, num_x, num_kv, queries, kv_pool, block_table, lengths, residual, out_weight, norm_gain, qkv_weight):
     group = queries.shape[1] // HEAD
     num_req, max_blocks = block_table.shape
     blocks, _, block, _ = kv_pool.shape
@@ -275,14 +274,11 @@
     anywhere = pl.BlockSpec(memory_space=pl.ANY)
     vmem = pl.BlockSpec(memory_space=pltpu.VMEM)
     dma = pltpu.SemaphoreType.DMA
-    return pl.pallas_call(
-        functools.partial(kernel, num_blk, inner, num_kv, group),
-        out_shape=(
-            jax.ShapeDtypeStruct((1, cols), BF16),
-            jax.ShapeDtypeStruct((1, out_cols), BF16),
-        ),
+    both = pl.pallas_call(
+        functools.partial(kernel, num_blk, num_x, num_kv, group),
+        out_shape=jax.ShapeDtypeStruct((1, cols + out_cols), BF16),
         in_specs=[anywhere] * 8,
-        out_specs=(vmem, vmem),
+        out_specs=vmem,
         scratch_shapes=[
             pltpu.VMEM(queries.shape, BF16),
             pltpu.VMEM(kv_pool.shape, BF16),
@@ -304,12 +300,21 @@
             pltpu.VMEM((num_blk * 8, HEAD), F32),
             pltpu.VMEM((num_kv, 1, width), F32),
             pltpu.VMEM((1, width), F32),
-            dma((8,)), dma((num_blk // inner,)), dma((num_blk // inner,)), dma, dma, dma((num_kv - 1,)), dma((num_kv - 1,)),
+            dma((8,)), pltpu.SemaphoreType.REGULAR, dma, dma, dma, dma, dma((num_kv - 1,)), dma((num_kv - 1,)),
         ],
         compiler_params=pltpu.CompilerParams(
             collective_id=0, has_side_effects=True, vmem_limit_bytes=60 * 1024 * 1024
         ),
     )(queries, kv_pool, block_table, lengths, residual, out_weight, norm_gain.reshape(-1, 128), qkv_weight)
+    return pl.pallas_call(
+        part,
+        out_shape=(
+            jax.ShapeDtypeStruct((1, cols), BF16),
+            jax.ShapeDtypeStruct((1, out_cols), BF16),
+        ),
+        in_specs=[vmem],
+        out_specs=(vmem, vmem),
+    )(both)
 
 
 def solution(mesh):
@@ -324,7 +329,7 @@
         P(None, "kv"),
     )
     return jax.shard_map(
-        functools.partial(per_device, mesh.shape["blk"], INNER, mesh.shape["kv"]),
+        functools.partial(per_device, mesh.shape["blk"], CHIPS_X, mesh.shape["kv"]),
         mesh=mesh,
         in_specs=placed,
         out_specs=(P("blk", "kv"), P("blk", "kv")),

time: 35.8 us -> 34.4 us (0.961)
  local copies, waits for them, and re-layouts: 2.49 us -> 0 us
  Pallas kernels: 32.5 us -> 33.6 us
    unnamed x2 -> x0, local copies, waits for them, and re-layouts: 2.49 us -> none
    pallas_call x1 -> x2, Pallas kernels: 32.5 us -> 33.6 us  [the longest x1 32.3 us: per_device(): pl.pallas_call(functools.partial(kernel, num_blk, num_x, num_kv, group),...]
where the time goes in v3:
time: 34.4 us; the launch traced here: 34.3 us
  Pallas kernels  33.6 us (98%)
  between operations  0.64 us (2%)
    pallas_call x1, Pallas kernels, per_device(): pl.pallas_call(functools.partial(kernel, num_blk, num_x, num_kv, group),...  32.3 us
    pallas_call x1, Pallas kernels, per_device(): pl.pallas_call(part, out_shape=(jax.ShapeDtypeStruct((1, cols), BF16), ja...  1.28 us

profile of v3, /device:TPU:1, one launch (start us, length us, event | category | flops | bytes accessed | tf_op | source)
XLA Modules:
  0.0 34.3 jit_solution(15894618745051863204)
XLA Ops:
  0.6 32.3 %shard_map.95.both_ref = bf16[1,1536]{1,0:T(2,128)(2,1)} custom-call(bf16[1,640]{1,0:T(2,128)(2,1)} %q_hbm.1, bf16[128,2,64,128]{3,2,1,0:T(8,128)(2,1)} %kv_hbm.1, s32[64,256]{1,0:T(8,128)} %table_hbm.1, s32[64]{0:T(128)} %len_hbm.1, bf16[1,640]{1,0:T(2,128)(2,1)} %res_hbm.1, bf16[640,2560]{1,0:T(8,128)(2,1)} %wo_hbm.1, bf16[20,128]{1,0:T(8,128)(2,1)} %bitcast.1, ...), custom_call_target="tpu_custom_call" | custom-call | tf_op jit(solution)/shard_map/pallas_call | solution.py:277
  33.0 1.3 %shard_map.96 = (bf16[1,640]{1,0:T(2,128)(2,1)}, bf16[1,896]{1,0:T(2,128)(2,1)}) custom-call(bf16[1,1536]{1,0:T(2,128)(2,1)} %shard_map.95.both_ref), custom_call_target="tpu_custom_call" | custom-call | tf_op jit(solution)/shard_map/pallas_call | solution.py:309

commit v4 on v3

--- a/solution.py
+++ b/solution.py
@@ -36,7 +36,7 @@
     both_ref,
     q_v, kv_v, table_v, len_s, res_v, wo_v, gain_v, wq_v,
     qall, code_v, expand, count8, qblk, outs, msgf, msg, recv, recvf, hbuf, hsum,
-    local_sem, ready, qs_sem, qr_sem, ms_sem, mr_sem, hs_sem, hr_sem,
+    local_sem, qs_sem, qr_sem, ms_sem, mr_sem, hs_sem, hr_sem,
 ):
     me = lax.axis_index("blk")
     kv = lax.axis_index("kv")
@@ -54,9 +54,6 @@
 
     others = [(a, b, c) for a in range(num_z) for b in range(num_x) for c in range(2)][1:]
     others.sort(key=hops, reverse=True)
-    plane = [k for k in others if k[0] == 0]
-    column = [k for k in others if k[1:] == (0, 0)]
-    rest = [k for k in others if k not in plane and k not in column]
     num_req = qall.shape[0]
     blocks = kv_v.shape[0]
     block = kv_v.shape[2]
@@ -69,12 +66,14 @@
     ]
     loads = [pltpu.make_async_copy(a, b, local_sem.at[i]) for i, (a, b) in enumerate(pairs)]
 
+    sent = pl.ds(0, 6)
+    qall[...] = jnp.zeros_like(qall)
     barrier = pltpu.get_barrier_semaphore()
     loads[0].start()
     loads[1].start()
     loads[2].start()
 
-    for k in column + plane:
+    for k in others:
         pl.semaphore_signal(barrier, inc=1, device_id={"blk": peer(k)}, device_id_type=MESH)
     for k in range(1, num_kv):
         pl.semaphore_signal(
@@ -128,25 +127,19 @@
 
     lax.fori_loop(0, blocks // 2, widen, 0, unroll=4)
 
-    pl.semaphore_wait(barrier, len(column) + len(plane) + num_kv - 1)
-
-    for k in plane:
-        pl.semaphore_signal(ready, inc=1, device_id={"blk": peer(k)}, device_id_type=MESH)
+    pl.semaphore_wait(barrier, num_blk - 1 + num_kv - 1)
 
     def send_query(k):
         pltpu.make_async_remote_copy(
-            src_ref=qall.at[me], dst_ref=qall.at[me], send_sem=qs_sem, recv_sem=qr_sem,
+            src_ref=qall.at[me, sent], dst_ref=qall.at[me, sent], send_sem=qs_sem, recv_sem=qr_sem,
             device_id={"blk": peer(k)}, device_id_type=MESH,
         ).start()
 
-    for k in column + plane:
-        send_query(k)
-    pl.semaphore_wait(ready, len(plane))
-    for k in rest:
+    for k in others:
         send_query(k)
     loads[3].wait()
     rows63 = pl.ds(0, num_blk - 1)
-    pltpu.make_async_copy(qall.at[rows63], qall.at[rows63], qr_sem).wait()
+    pltpu.make_async_copy(qall.at[rows63, sent], qall.at[rows63, sent], qr_sem).wait()
 
     flat = qall[...].astype(F32).reshape(num_req * 8, HEAD).astype(BF16)
     qblk[...] = dot(expand[...], flat).astype(BF16)
@@ -184,8 +177,7 @@
         outs[g * rows : (g + 1) * rows, :] = dot(weights[g], v)
 
     lane_r = lax.broadcasted_iota(jnp.int32, (num_req, 128), 1)
-    tops = jnp.zeros((num_req, 128), F32)
-    sums = jnp.zeros((num_req, 128), F32)
+    stats = jnp.zeros((num_req, 128), F32)
     for h in range(group):
         high = jnp.where(owns, bmax[h : h + 1, :], NEG)
         top = jnp.max(high, axis=1, keepdims=True).astype(BF16).astype(F32)
@@ -195,30 +187,30 @@
         o_hi, o_lo = split(outs[pl.ds(h, blocks, stride=8), :])
         acc = dot(w_hi, o_hi) + dot(w_hi, o_lo) + dot(w_lo, o_hi)
         msgf[pl.ds(h, num_req, stride=8), :] = acc
-        tops = jnp.where(lane_r == h, top, tops)
-        sums = jnp.where(lane_r == h, total, sums)
-    sum_hi = sums.astype(BF16).astype(F32)
-    msgf[pl.ds(group, num_req, stride=8), :] = tops
-    msgf[pl.ds(group + 1, num_req, stride=8), :] = sum_hi
-    msgf[pl.ds(group + 2, num_req, stride=8), :] = sums - sum_hi
+        sum_hi = total.astype(BF16).astype(F32)
+        stats = jnp.where(lane_r == h, top, stats)
+        stats = jnp.where(lane_r == h + 8, sum_hi, stats)
+        stats = jnp.where(lane_r == h + 16, total - sum_hi, stats)
+    msgf[pl.ds(group, num_req, stride=8), :] = stats
     msg[...] = msgf[...].reshape(num_req, 8, 128).astype(BF16)
     recv[me] = msg[me]
 
     for k in others:
         to = peer(k)
         pltpu.make_async_remote_copy(
-            src_ref=msg.at[to], dst_ref=recv.at[me], send_sem=ms_sem, recv_sem=mr_sem,
+            src_ref=msg.at[to, sent], dst_ref=recv.at[me, sent], send_sem=ms_sem, recv_sem=mr_sem,
             device_id={"blk": to}, device_id_type=MESH,
         ).start()
     for load in loads[4:]:
         load.wait()
-    pltpu.make_async_copy(recv.at[rows63], recv.at[rows63], mr_sem).wait()
+    pltpu.make_async_copy(recv.at[rows63, sent], recv.at[rows63, sent], mr_sem).wait()
 
     gain = gain_v[...].astype(F32)
     gain = jnp.concatenate([gain[i : i + 1, :] for i in range(width // 128)], axis=1)
     recvf[...] = recv[...].astype(F32).reshape(num_blk * 8, 128)
-    tops = recvf[pl.ds(group, num_blk, stride=8), :]
-    sums = recvf[pl.ds(group + 1, num_blk, stride=8), :] + recvf[pl.ds(group + 2, num_blk, stride=8), :]
+    stats = recvf[pl.ds(group, num_blk, stride=8), :]
+    sums = pltpu.roll(stats, 128 - 8, 1) + pltpu.roll(stats, 128 - 16, 1)
+    tops = jnp.where(lane_r < group, stats, 0.0)
     w = jnp.exp(tops - jnp.max(tops, axis=0, keepdims=True))
     total = jnp.sum(w * sums, axis=0, keepdims=True)
     heads = []
@@ -254,8 +246,8 @@
 
     for hop in hops_y:
         hop.wait_send()
-    pltpu.make_async_copy(qall.at[rows63], qall.at[rows63], qs_sem).wait()
-    pltpu.make_async_copy(recv.at[rows63], recv.at[rows63], ms_sem).wait()
+    pltpu.make_async_copy(qall.at[rows63, sent], qall.at[rows63, sent], qs_sem).wait()
+    pltpu.make_async_copy(recv.at[rows63, sent], recv.at[rows63, sent], ms_sem).wait()
 
 
 def part(both_ref, stream_ref, next_ref):
@@ -300,7 +292,7 @@
             pltpu.VMEM((num_blk * 8, HEAD), F32),
             pltpu.VMEM((num_kv, 1, width), F32),
             pltpu.VMEM((1, width), F32),
-            dma((8,)), pltpu.SemaphoreType.REGULAR, dma, dma, dma, dma, dma((num_kv - 1,)), dma((num_kv - 1,)),
+            dma((8,)), dma, dma, dma, dma, dma((num_kv - 1,)), dma((num_kv - 1,)),
         ],
         compiler_params=pltpu.CompilerParams(
             collective_id=0, has_side_effects=True, vmem_limit_bytes=60 * 1024 * 1024

time: 34.4 us -> 33.1 us (0.962)
  Pallas kernels: 33.6 us -> 32.3 us
    pallas_call x1, Pallas kernels: 32.3 us -> 31 us  [per_device(): pl.pallas_call(functools.partial(kernel, num_blk, num_x, num_kv, group),...]
where the time goes in v4:
time: 33.1 us; the launch traced here: 32.9 us
  Pallas kernels  32.3 us (98%)
  between operations  0.64 us (2%)
    pallas_call x1, Pallas kernels, per_device(): pl.pallas_call(functools.partial(kernel, num_blk, num_x, num_kv, group),...  31 us
    pallas_call x1, Pallas kernels, per_device(): pl.pallas_call(part, out_shape=(jax.ShapeDtypeStruct((1, cols), BF16), ja...  1.28 us

profile of v4, /device:TPU:1, one launch (start us, length us, event | category | flops | bytes accessed | tf_op | source)
XLA Modules:
  0.0 32.9 jit_solution(1996950580409060734)
XLA Ops:
  0.6 31.0 %shard_map.95.both_ref = bf16[1,1536]{1,0:T(2,128)(2,1)} custom-call(bf16[1,640]{1,0:T(2,128)(2,1)} %q_hbm.1, bf16[128,2,64,128]{3,2,1,0:T(8,128)(2,1)} %kv_hbm.1, s32[64,256]{1,0:T(8,128)} %table_hbm.1, s32[64]{0:T(128)} %len_hbm.1, bf16[1,640]{1,0:T(2,128)(2,1)} %res_hbm.1, bf16[640,2560]{1,0:T(8,128)(2,1)} %wo_hbm.1, bf16[20,128]{1,0:T(8,128)(2,1)} %bitcast.1, ...), custom_call_target="tpu_custom_call" | custom-call | tf_op jit(solution)/shard_map/pallas_call | solution.py:269
  31.6 1.3 %shard_map.96 = (bf16[1,640]{1,0:T(2,128)(2,1)}, bf16[1,896]{1,0:T(2,128)(2,1)}) custom-call(bf16[1,1536]{1,0:T(2,128)(2,1)} %shard_map.95.both_ref), custom_call_target="tpu_custom_call" | custom-call | tf_op jit(solution)/shard_map/pallas_call | solution.py:301

commit v5 on v4

--- a/solution.py
+++ b/solution.py
@@ -35,7 +35,7 @@
     q_hbm, kv_hbm, table_hbm, len_hbm, res_hbm, wo_hbm, gain_hbm, wq_hbm,
     both_ref,
     q_v, kv_v, table_v, len_s, res_v, wo_v, gain_v, wq_v,
-    qall, code_v, expand, count8, qblk, outs, msgf, msg, recv, recvf, hbuf, hsum,
+    qall, code_v, expand, count8, outs, msgf, msg, recv, recvf, hbuf, hsum,
     local_sem, qs_sem, qr_sem, ms_sem, mr_sem, hs_sem, hr_sem,
 ):
     me = lax.axis_index("blk")
@@ -69,9 +69,6 @@
     sent = pl.ds(0, 6)
     qall[...] = jnp.zeros_like(qall)
     barrier = pltpu.get_barrier_semaphore()
-    loads[0].start()
-    loads[1].start()
-    loads[2].start()
 
     for k in others:
         pl.semaphore_signal(barrier, inc=1, device_id={"blk": peer(k)}, device_id_type=MESH)
@@ -79,7 +76,7 @@
         pl.semaphore_signal(
             barrier, inc=1, device_id={"kv": lax.rem(kv + k, num_kv)}, device_id_type=MESH
         )
-    for load in loads[3:]:
+    for load in loads:
         load.start()
 
     loads[0].wait()
@@ -142,7 +139,7 @@
     pltpu.make_async_copy(qall.at[rows63, sent], qall.at[rows63, sent], qr_sem).wait()
 
     flat = qall[...].astype(F32).reshape(num_req * 8, HEAD).astype(BF16)
-    qblk[...] = dot(expand[...], flat).astype(BF16)
+    asked = dot(expand[...], flat).astype(BF16)
 
     rows = 32
     toks = 4 * block
@@ -154,7 +151,7 @@
     groups = blocks // 4
     scores = []
     for g in range(groups):
-        q = qblk[g * rows : (g + 1) * rows, :]
+        q = asked[g * rows : (g + 1) * rows, :]
         k = kv_v[g * 4 : (g + 1) * 4, 0].reshape(toks, HEAD)
         scores.append(lax.dot_general(q, k, (((1,), (1,)), ((), ())), preferred_element_type=F32))
     bmax = jnp.zeros((8, 128), F32)
@@ -268,7 +265,7 @@
     dma = pltpu.SemaphoreType.DMA
     both = pl.pallas_call(
         functools.partial(kernel, num_blk, num_x, num_kv, group),
-        out_shape=jax.ShapeDtypeStruct((1, cols + out_cols), BF16),
+        out_shape=pltpu.VMEM((1, cols + out_cols), BF16),
         in_specs=[anywhere] * 8,
         out_specs=vmem,
         scratch_shapes=[
@@ -284,7 +281,6 @@
             pltpu.VMEM((blocks, 128), F32),
             pltpu.VMEM((blocks * 8, num_req * 8), BF16),
             pltpu.VMEM((blocks * 8, 128), jnp.int32),
-            pltpu.VMEM((blocks * 8, HEAD), BF16),
             pltpu.VMEM((blocks * 8, HEAD), F32),
             pltpu.VMEM((num_req * 8, HEAD), F32),
             pltpu.VMEM((num_req, 8, HEAD), BF16),
@@ -306,7 +302,7 @@
         ),
         in_specs=[vmem],
         out_specs=(vmem, vmem),
-    )(both)
+    )(pltpu.with_memory_space_constraint(both, pltpu.VMEM))
 
 
 def solution(mesh):

time: 33.1 us -> 31.7 us (0.958)
  Pallas kernels: 32.3 us -> 31 us
    pallas_call x1, Pallas kernels: 1.28 us -> 0.59 us  [per_device(): pl.pallas_call(part, out_shape=(jax.ShapeDtypeStruct((1, cols), BF16), ja...]
    pallas_call x1, Pallas kernels: 31 us -> 30.4 us  [per_device(): pl.pallas_call(functools.partial(kernel, num_blk, num_x, num_kv, group),...]
where the time goes in v5:
time: 31.7 us; the launch traced here: 31.6 us
  Pallas kernels  31 us (98%)
  between operations  0.64 us (2%)
    pallas_call x1, Pallas kernels, per_device(): pl.pallas_call(functools.partial(kernel, num_blk, num_x, num_kv, group),...  30.4 us

profile of v5, /device:TPU:1, one launch (start us, length us, event | category | flops | bytes accessed | tf_op | source)
XLA Modules:
  0.0 31.6 jit_solution(187341252816467970)
XLA Ops:
  0.6 30.4 %shard_map.95.both_ref = bf16[1,1536]{1,0:T(2,128)(2,1)S(1)} custom-call(bf16[1,640]{1,0:T(2,128)(2,1)} %q_hbm.1, bf16[128,2,64,128]{3,2,1,0:T(8,128)(2,1)} %kv_hbm.1, s32[64,256]{1,0:T(8,128)} %table_hbm.1, s32[64]{0:T(128)} %len_hbm.1, bf16[1,640]{1,0:T(2,128)(2,1)} %res_hbm.1, bf16[640,2560]{1,0:T(8,128)(2,1)} %wo_hbm.1, bf16[20,128]{1,0:T(8,128)(2,1)} %bitcast.1, ...), custom_call_target="tpu_custom_call" | custom-call | tf_op jit(solution)/shard_map/pallas_call | solution.py:266
  31.0 0.6 %shard_map.96 = (bf16[1,640]{1,0:T(2,128)(2,1)}, bf16[1,896]{1,0:T(2,128)(2,1)}) custom-call(bf16[1,1536]{1,0:T(2,128)(2,1)S(1)} %shard_map.95.both_ref), custom_call_target="tpu_custom_call" | custom-call | tf_op jit(solution)/shard_map/pallas_call | solution.py:297

commit v6 on v5

--- a/solution.py
+++ b/solution.py
@@ -138,7 +138,7 @@
     rows63 = pl.ds(0, num_blk - 1)
     pltpu.make_async_copy(qall.at[rows63, sent], qall.at[rows63, sent], qr_sem).wait()
 
-    flat = qall[...].astype(F32).reshape(num_req * 8, HEAD).astype(BF16)
+    flat = qall[...].reshape(num_req * 8, HEAD)
     asked = dot(expand[...], flat).astype(BF16)
 
     rows = 32
@@ -221,7 +221,7 @@
     hbuf[kv, :, own] = hbuf[kv, :, own] + res_v[...].astype(F32)
 
     hops_y = []
-    for j in range(1, num_kv):
+    for j in sorted(range(1, num_kv), key=lambda j: -min(j, num_kv - j)):
         hops_y.append(pltpu.make_async_remote_copy(
             src_ref=hbuf.at[kv], dst_ref=hbuf.at[kv], send_sem=hs_sem.at[j - 1], recv_sem=hr_sem.at[j - 1],
             device_id={"kv": lax.rem(kv + j, num_kv)}, device_id_type=MESH,

time: 31.7 us -> 31.6 us (level)
  no operation moved by 1% of the time
where the time goes in v6:
time: 31.6 us; the launch traced here: 31.5 us
  Pallas kernels  30.8 us (97%)
  between operations  0.64 us (2%)
    pallas_call x1, Pallas kernels, per_device(): pl.pallas_call(functools.partial(kernel, num_blk, num_x, num_kv, group),...  30.3 us

profile of v6, /device:TPU:1, one launch (start us, length us, event | category | flops | bytes accessed | tf_op | source)
XLA Modules:
  0.0 31.5 jit_solution(5374908916928070060)
XLA Ops:
  0.6 30.3 %shard_map.95.both_ref = bf16[1,1536]{1,0:T(2,128)(2,1)S(1)} custom-call(bf16[1,640]{1,0:T(2,128)(2,1)} %q_hbm.1, bf16[128,2,64,128]{3,2,1,0:T(8,128)(2,1)} %kv_hbm.1, s32[64,256]{1,0:T(8,128)} %table_hbm.1, s32[64]{0:T(128)} %len_hbm.1, bf16[1,640]{1,0:T(2,128)(2,1)} %res_hbm.1, bf16[640,2560]{1,0:T(8,128)(2,1)} %wo_hbm.1, bf16[20,128]{1,0:T(8,128)(2,1)} %bitcast.1, ...), custom_call_target="tpu_custom_call" | custom-call | tf_op jit(solution)/shard_map/pallas_call | solution.py:266
  30.9 0.6 %shard_map.96 = (bf16[1,640]{1,0:T(2,128)(2,1)}, bf16[1,896]{1,0:T(2,128)(2,1)}) custom-call(bf16[1,1536]{1,0:T(2,128)(2,1)S(1)} %shard_map.95.both_ref), custom_call_target="tpu_custom_call" | custom-call | tf_op jit(solution)/shard_map/pallas_call | solution.py:297

commit v7 on v5

--- a/solution.py
+++ b/solution.py
@@ -200,6 +200,9 @@
         ).start()
     for load in loads[4:]:
         load.wait()
+    own = pl.ds(pl.multiple_of(kv * cols, 128), cols)
+    hsum[...] = jnp.zeros_like(hsum)
+    hsum[:, own] = res_v[...].astype(F32)
     pltpu.make_async_copy(recv.at[rows63, sent], recv.at[rows63, sent], mr_sem).wait()
 
     gain = gain_v[...].astype(F32)
@@ -216,18 +219,19 @@
         heads.append(acc / total[:, h : h + 1])
     attn = jnp.concatenate(heads, axis=1)
     attn8 = jnp.broadcast_to(attn, (8, group * HEAD)).astype(BF16)
-    hbuf[kv] = dot(attn8, wo_v[...])[:1, :]
-    own = pl.ds(pl.multiple_of(kv * cols, 128), cols)
-    hbuf[kv, :, own] = hbuf[kv, :, own] + res_v[...].astype(F32)
-
     hops_y = []
-    for j in range(1, num_kv):
-        hops_y.append(pltpu.make_async_remote_copy(
-            src_ref=hbuf.at[kv], dst_ref=hbuf.at[kv], send_sem=hs_sem.at[j - 1], recv_sem=hr_sem.at[j - 1],
-            device_id={"kv": lax.rem(kv + j, num_kv)}, device_id_type=MESH,
-        ))
-    for hop in hops_y:
-        hop.start()
+    half = width // 2
+    for part in range(2):
+        at = pl.ds(part * half, half)
+        hbuf[kv, :, at] = dot(attn8, wo_v[:, at])[:1, :] + hsum[:, at]
+        for j in range(1, num_kv):
+            sem = part * (num_kv - 1) + j - 1
+            hops_y.append(pltpu.make_async_remote_copy(
+                src_ref=hbuf.at[kv, :, at], dst_ref=hbuf.at[kv, :, at],
+                send_sem=hs_sem.at[sem], recv_sem=hr_sem.at[sem],
+                device_id={"kv": lax.rem(kv + j, num_kv)}, device_id_type=MESH,
+            ))
+            hops_y[-1].start()
     for hop in hops_y:
         hop.wait_recv()
 
@@ -288,7 +292,7 @@
             pltpu.VMEM((num_blk * 8, HEAD), F32),
             pltpu.VMEM((num_kv, 1, width), F32),
             pltpu.VMEM((1, width), F32),
-            dma((8,)), dma, dma, dma, dma, dma((num_kv - 1,)), dma((num_kv - 1,)),
+            dma((8,)), dma, dma, dma, dma, dma((2 * num_kv - 2,)), dma((2 * num_kv - 2,)),
         ],
         compiler_params=pltpu.CompilerParams(
             collective_id=0, has_side_effects=True, vmem_limit_bytes=60 * 1024 * 1024

time: 31.7 us -> 31.8 us (level)
  no operation moved by 1% of the time
where the time goes in v7:
time: 31.8 us; the launch traced here: 31.7 us
  Pallas kernels  31.1 us (98%)
  between operations  0.64 us (2%)
    pallas_call x1, Pallas kernels, per_device(): pl.pallas_call(functools.partial(kernel, num_blk, num_x, num_kv, group),...  30.5 us

profile of v7, /device:TPU:1, one launch (start us, length us, event | category | flops | bytes accessed | tf_op | source)
XLA Modules:
  0.0 31.7 jit_solution(12566626768792531769)
XLA Ops:
  0.6 30.5 %shard_map.95.both_ref = bf16[1,1536]{1,0:T(2,128)(2,1)S(1)} custom-call(bf16[1,640]{1,0:T(2,128)(2,1)} %q_hbm.1, bf16[128,2,64,128]{3,2,1,0:T(8,128)(2,1)} %kv_hbm.1, s32[64,256]{1,0:T(8,128)} %table_hbm.1, s32[64]{0:T(128)} %len_hbm.1, bf16[1,640]{1,0:T(2,128)(2,1)} %res_hbm.1, bf16[640,2560]{1,0:T(8,128)(2,1)} %wo_hbm.1, bf16[20,128]{1,0:T(8,128)(2,1)} %bitcast.1, ...), custom_call_target="tpu_custom_call" | custom-call | tf_op jit(solution)/shard_map/pallas_call | solution.py:270
  31.1 0.6 %shard_map.96 = (bf16[1,640]{1,0:T(2,128)(2,1)}, bf16[1,896]{1,0:T(2,128)(2,1)}) custom-call(bf16[1,1536]{1,0:T(2,128)(2,1)S(1)} %shard_map.95.both_ref), custom_call_target="tpu_custom_call" | custom-call | tf_op jit(solution)/shard_map/pallas_call | solution.py:301
